TPU v7x, 1024 devices: a whole 8x8x8 slice. The times are simulated.
1024 devices in a mesh: phase: 32 (over x, z_hi, core), ctx: 8 (over y), tp: 4 (over z_lo).
Axes of the slice: x: 8, y: 8, z: 8 (z_hi: 2, z_lo: 4; z = z_hi * 4 + z_lo), core: 2. Of those that a mesh axis runs over, the one named last changes fastest.
Arguments:
- queries: bfloat16 [32, 1024, 4096], P('phase', 'ctx', 'tp'), may hold values from -8 to 8
- keys: bfloat16 [32, 1024, 512], P('phase', 'ctx', 'tp'), may hold values from -8 to 8
- values: bfloat16 [32, 1024, 512], P('phase', 'ctx', 'tp'), may hold values from -6 to 6
- seg_ids: int32 [32, 1024], P('phase'), may hold values from 0 to 3, never falling along the last dimension, each value on 1 to 512 neighbouring positions
- out_weight: bfloat16 [4096, 8192], P('tp', 'ctx'), may hold values from -0.5 to 0.5
- embedded: bfloat16 [1024, 8192], P('tp', 'ctx'), may hold values from -6 to 6
- hidden_prev: bfloat16 [32, 1024, 8192], P('phase', 'tp', 'ctx'), may hold values from -6 to 6
Outputs:
- hidden_next: bfloat16 [32, 1024, 8192], P('phase', 'tp', 'ctx')
Inputs may be any that keep to these rules, and one draw needn't show every extreme that they name: `seg_ids`: within each section the segment number never falls; a segment holds at most 512 tokens.
All inputs are finite; a program needn't handle non-finite values.
Results may differ from a plain program's by a relative error of at most 0.015.
Values may be sent and summed in bfloat16 or wider, within the bound.
A program may use at most 32 MiB of HBM per device.

v0:
```python
import jax
import jax.numpy as jnp
from jax import lax
from jax.sharding import PartitionSpec as P

HEAD_DIM = 128


def passed_along(shard, axis, by):
    peers = lax.axis_size(axis)
    pairs = [(i, i + by) for i in range(peers) if 0 <= i + by < peers]
    return lax.ppermute(shard, axis, pairs)


def on_device(queries, keys, values, seg_ids, out_weight, embedded, hidden_prev):
    shard_rows = queries.shape[1]
    kv_local = keys.shape[2] // HEAD_DIM
    heads_local = queries.shape[2] // HEAD_DIM
    group_size = heads_local // kv_local
    kv_width = kv_local * HEAD_DIM
    score_scale = HEAD_DIM ** (-0.5)
    ctx_place = lax.axis_index("ctx")
    offset = ctx_place * shard_rows
    query_grid = queries[0].reshape(shard_rows, kv_local, group_size, HEAD_DIM)
    segment_row = seg_ids[0]
    query_places = offset + jnp.arange(shard_rows, dtype=jnp.int32)
    query_segs = lax.dynamic_slice_in_dim(segment_row, offset, shard_rows)
    stacked = jnp.concatenate((keys, values), axis=2)
    pieces = lax.all_gather(stacked, "ctx", axis=1, tiled=True)
    length = pieces.shape[1]
    key_grid = pieces[0, :, :kv_width].reshape(length, kv_local, HEAD_DIM)
    value_grid = pieces[0, :, kv_width:].reshape(length, kv_local, HEAD_DIM)
    key_places = jnp.arange(length, dtype=jnp.int32)
    allowed = (query_places[:, None] >= key_places[None, :]) & (key_places[None, :] >= 0)
    allowed = allowed & (query_segs[:, None] == segment_row[None, :])
    mask_grid = allowed[:, None, None, :]
    scores = (
        jnp.einsum("qkgd,nkd->qkgn", query_grid, key_grid, preferred_element_type=jnp.float32)
        * score_scale
    )
    running_max = jnp.full((shard_rows, kv_local, group_size), -1e30, jnp.float32)
    new_max = jnp.maximum(running_max, jnp.max(jnp.where(mask_grid, scores, -1e30), axis=3))
    probs = jnp.where(mask_grid, jnp.exp(scores - new_max[..., None]), 0.0)
    new_sum = jnp.sum(probs, axis=3)
    new_out = jnp.einsum(
        "qkgn,nkd->qkgd", probs.astype(jnp.bfloat16), value_grid, preferred_element_type=jnp.float32
    )
    attended = (
        (new_out / new_sum[..., None])
        .reshape(shard_rows, heads_local * HEAD_DIM)
        .astype(jnp.bfloat16)
    )
    partial_value = jnp.dot(
        lax.all_gather(attended, "ctx", axis=0, tiled=True),
        out_weight,
        preferred_element_type=jnp.float32,
    )
    summed = lax.psum_scatter(
        partial_value.astype(jnp.bfloat16), "tp", scatter_dimension=0, tiled=True
    ).astype(jnp.float32)
    arrived = passed_along(hidden_prev, "phase", 1)
    resid_in = jnp.where(lax.axis_index("phase") == 0, embedded, arrived[0])
    return (resid_in.astype(jnp.float32) + summed).astype(jnp.bfloat16)[None]


def solution(mesh):
    return jax.shard_map(
        on_device,
        mesh=mesh,
        in_specs=(
            P("phase", "ctx", "tp"),
            P("phase", "ctx", "tp"),
            P("phase", "ctx", "tp"),
            P("phase", None),
            P("tp", "ctx"),
            P("tp", "ctx"),
            P("phase", "tp", "ctx"),
        ),
        out_specs=P("phase", "tp", "ctx"),
        check_vma=False,
    )
```

profile of v0, /device:TPU:14, one launch (start us, length us, event | category | flops | bytes accessed | tf_op | source)
XLA Modules:
  0.0 175.0 jit_solution(10358906510509117588)
XLA Ops:
  6.5 0.0 copy-start
  6.5 0.0 all-gather.2.cloned.1.call-start
  6.5 0.9 pad_maximum_fusion
  7.5 27.8 %all_gather.6 = bf16[1,1024,256]{2,1,0:T(8,128)(2,1)S(1)} all-gather(bf16[1,128,256]{2,1,0:T(8,128)(2,1)S(1)} %pad_maximum_fusion), channel_id=1, replica_groups=mesh['phase'=32,'ctx'=8,'tp'=4] {'ctx'}, dimensions={1}, use_global_device_ids=true | all-gather | bytes 589824 | tf_op jit(solution)/shard_map/all_gather | solution.py:29
  35.3 1.0 copy.14
  36.3 0.7 dynamic-slice_bitcast_fusion
  36.9 0.9 fusion.19
  37.8 0.8 fusion
  38.6 0.9 fusion.3
  39.5 1.7 fusion.15
  41.1 0.0 all-gather.2.cloned.1.call-update
  41.2 0.0 copy-start.1
  41.2 0.0 reduce-scatter.2.cloned.1.call-start
  41.2 61.1 %all-gather.2.cloned.1.call-done = bf16[1024,1024]{0,1:T(8,128)(2,1)} async-done(((bf16[128,1024]{0,1:T(8,128)(2,1)}), bf16[1024,1024]{0,1:T(8,128)(2,1)}) %all-gather.2.cloned.1.call-update) | async-done | bytes 2097168 | tf_op jit(solution)/shard_map/all_gather | solution.py:54
  102.4 0.0 copy-done
  102.4 5.3 %convolution_convert_fusion = bf16[1024,1024]{1,0:T(8,128)(2,1)} fusion(bf16[1024,1024]{0,1:T(8,128)(2,1)} %all-gather.2.cloned.1.call-done, bf16[1024,1024]{1,0:T(8,128)(2,1)S(1)} %copy-done), kind=kOutput, calls=%fused_computation.10 | convolution fusion | flops 2148532224 | bytes 6291456 | tf_op jit(solution)/shard_map/dot_general | solution.py:53
  107.7 0.0 reduce-scatter.2.cloned.1.call-update
  107.7 1.9 %collective-permute-start = (bf16[1,256,1024]{2,1,0:T(8,128)(2,1)}, bf16[1,256,1024]{2,1,0:T(8,128)(2,1)S(1)}, u32[]{:S(2)}, u32[]{:S(2)}) collective-permute-start(bf16[1,256,1024]{2,1,0:T(8,128)(2,1)} %param.13), channel_id=1, source_target_pairs={{0,32},{32,64},{64,96},{96,128},{128,160},{160,192},{192,224},{224... | collective-permute-start | bytes 1572872 | tf_op jit(solution)/shard_map/ppermute | solution.py:12
  109.6 17.4 %collective-permute-done = bf16[1,256,1024]{2,1,0:T(8,128)(2,1)S(1)} collective-permute-done((bf16[1,256,1024]{2,1,0:T(8,128)(2,1)}, bf16[1,256,1024]{2,1,0:T(8,128)(2,1)S(1)}, u32[]{:S(2)}, u32[]{:S(2)}) %collective-permute-start) | collective-permute-done | bytes 524320 | tf_op jit(solution)/shard_map/ppermute | solution.py:12
  127.1 39.0 %reduce-scatter.2.cloned.1.call-done = bf16[256,1024]{1,0:T(8,128)(2,1)} async-done(((bf16[1024,1024]{1,0:T(8,128)(2,1)}), bf16[256,1024]{1,0:T(8,128)(2,1)}) %reduce-scatter.2.cloned.1.call-update) | async-done | bytes 524304 | tf_op jit(solution)/shard_map/reduce_scatter | solution.py:58
  166.1 0.0 copy-done.1
  166.1 2.1 %fusion.18 = bf16[1,256,1024]{2,1,0:T(8,128)(2,1)} fusion(bf16[256,1024]{1,0:T(8,128)(2,1)} %reduce-scatter.2.cloned.1.call-done, bf16[256,1024]{1,0:T(8,128)(2,1)S(1)} %copy-done.1, bf16[1,256,1024]{2,1,0:T(8,128)(2,1)S(1)} %collective-permute-done, pred[]{:T(512)S(6)} %eq.24), kind=kLoop, calls=%fused_computation.15 | loop fusion | flops 1310720 | bytes 2097153 | tf_op jit(solution)/shard_map/broadcast_in_dim | solution.py:63
  (2 shorter events, 0.0 us)
Async XLA Ops:
  6.5 95.8 %copy-start = (bf16[1024,1024]{1,0:T(8,128)(2,1)S(1)}, bf16[1024,1024]{1,0:T(8,128)(2,1)}, u32[]{:S(2)}) copy-start(bf16[1024,1024]{1,0:T(8,128)(2,1)} %param.11) | copy-start | bytes 6291460
  6.5 95.8 %all-gather.2.cloned.1.call-start = ((), (), s32[]{:S(2)}) async-start(), calls=%async_computation.1 | async-start | bytes 2359296 | tf_op jit(solution)/shard_map/all_gather | solution.py:54
  41.2 124.9 %copy-start.1 = (bf16[256,1024]{1,0:T(8,128)(2,1)S(1)}, bf16[256,1024]{1,0:T(8,128)(2,1)}, u32[]{:S(2)}) copy-start(bf16[256,1024]{1,0:T(8,128)(2,1)} %param.12) | copy-start | bytes 1572868
  41.2 124.9 %reduce-scatter.2.cloned.1.call-start = ((), (), s32[]{:S(2)}) async-start(), calls=%async_computation.2 | async-start | bytes 2621440 | tf_op jit(solution)/shard_map/reduce_scatter | solution.py:58
  107.7 19.4 %collective-permute-start = (bf16[1,256,1024]{2,1,0:T(8,128)(2,1)}, bf16[1,256,1024]{2,1,0:T(8,128)(2,1)S(1)}, u32[]{:S(2)}, u32[]{:S(2)}) collective-permute-start(bf16[1,256,1024]{2,1,0:T(8,128)(2,1)} %param.13), channel_id=1, source_target_pairs={{0,32},{32,64},{64,96},{96,128},{128,160},{160,192},{192,224},{224... | collective-permute-start | bytes 1572872 | tf_op jit(solution)/shard_map/ppermute | solution.py:12
Sparse Core Ops, SparseCore 0:
  41.3 61.0 all-gather.1
  107.8 58.2 reduce-scatter.1
where the time goes:
time: 176 us; the launch traced here: 175 us
  waiting for transfers between devices  118 us (67%)
  blocking collectives  27.8 us (16%)
  between operations  13.5 us (8%)
  matrix products  7.74 us (4%)
  other arithmetic  4.79 us (3%)
  starting transfers between devices  1.97 us (1%)
    all_gather x1, waiting for transfers between devices, on_device(): lax.all_gather(attended, 'ctx', axis=0, tiled=True)  61.1 us
    reduce_scatter x1, waiting for transfers between devices, on_device(): lax.psum_scatter(partial_value.astype(jnp.bfloat16), 'tp', scatter_dimens...  39 us
    all_gather x1, blocking collectives, on_device(): pieces = lax.all_gather(stacked, 'ctx', axis=1, tiled=True)  27.8 us
    ppermute x1, waiting for transfers between devices, passed_along(): return lax.ppermute(shard, axis, pairs)  17.4 us
    dot_general x1, matrix products, on_device(): jnp.dot(lax.all_gather(attended, 'ctx', axis=0, tiled=True), out_weight,...  5.32 us
  transfers between devices with their start and end apart: 3, of which 3 were waited for; matrix products, arithmetic and copies ran while one was open for 0% of the time, Pallas kernels for 0%

commit v1 on v0

v1 whole, which is shorter than its diff:
```python
import jax
import jax.numpy as jnp
from jax import lax
from jax.experimental import pallas as pl
from jax.experimental.pallas import tpu as pltpu
from jax.sharding import PartitionSpec as P

HEAD_DIM = 128
BLOCK = 128
RING = 8
GROUP = 4
PIECE = 64
MASKED = -1e30
LOG2_E = 1.4426950408889634
F32 = jnp.float32
BF16 = jnp.bfloat16


def kernel(
    q_ref, k_ref, v_ref, seg_ref, w_ref, emb_ref, hp_ref, out_ref,
    qbuf, kv, bias, astage, aall, wall, hbuf, acc,
    local_sem, kv_s, kv_r, q_s, q_r, wz_s, wz_r, wx_s, wx_r, sib_s, sib_r, hid_s, hid_r, az_s, az_r, ay_s, ay_r,
):
    p = lax.axis_index("phase")
    y = lax.axis_index("ctx")
    z = lax.axis_index("tp")
    x = lax.div(p, 4)
    zh = lax.rem(lax.div(p, 2), 2)
    core = lax.rem(p, 2)
    zring = zh * GROUP + z

    def ring(value):
        return lax.rem(value + 2 * RING, RING)

    def at_y(step):
        return {"phase": p, "ctx": ring(y + step), "tp": z}

    def at_x(step):
        return {"phase": lax.rem(p + 4 * step + 32, 32), "ctx": y, "tp": z}

    def at_zring(step):
        there = ring(zring + step)
        return {"phase": x * 4 + lax.div(there, GROUP) * 2 + core, "ctx": y, "tp": lax.rem(there, GROUP)}

    def at_z(place):
        return {"phase": p, "ctx": y, "tp": place}

    def at_phase(step):
        return {"phase": lax.rem(p + step + 32, 32), "ctx": y, "tp": z}

    sibling = {"phase": p + 1 - 2 * core, "ctx": y, "tp": z}

    def remote(src, dst, send, recv, where):
        return pltpu.make_async_remote_copy(
            src_ref=src, dst_ref=dst, send_sem=send, recv_sem=recv,
            device_id=where, device_id_type=pl.DeviceIdType.MESH,
        )

    barrier = pltpu.get_barrier_semaphore()
    greeted = [at_y(d) for d in range(1, RING)]
    greeted += [at_z(lax.rem(z + d, GROUP)) for d in range(1, GROUP)]
    greeted += [at_zring(d) for d in (1, -1, 2, -2)]
    greeted += [at_x(1), at_x(-1), sibling, at_phase(1), at_phase(-1)]
    for peer in greeted:
        pl.semaphore_signal(barrier, inc=1, device_id=peer, device_id_type=pl.DeviceIdType.MESH)

    k_in = pltpu.make_async_copy(k_ref, kv.at[y, 0], local_sem.at[0])
    v_in = pltpu.make_async_copy(v_ref, kv.at[y, 1], local_sem.at[1])
    q_in = pltpu.make_async_copy(
        q_ref.at[:, pl.ds(pl.multiple_of(y * HEAD_DIM, HEAD_DIM), HEAD_DIM)], qbuf.at[y], local_sem.at[2]
    )
    w_in = pltpu.make_async_copy(w_ref, wall.at[:, z], local_sem.at[3])
    k_in.start()
    v_in.start()
    q_in.start()
    w_in.start()

    @pl.when(p == 0)
    def _():
        pltpu.make_async_copy(emb_ref, hbuf, local_sem.at[4]).start()

    k_in.wait()
    v_in.wait()
    pl.semaphore_wait(barrier, len(greeted))

    sends = []

    def go(copy):
        copy.start()
        sends.append(copy)

    def kv_copy(way, hop):
        block = ring(y - hop + 1) if way == 0 else ring(y + hop - 1)
        part = kv.at[block] if hop < 4 else kv.at[block, way]
        return remote(part, part, kv_s.at[way, hop - 1], kv_r.at[way, hop - 1], at_y(1 if way == 0 else -1))

    kv_copies = {(way, hop): kv_copy(way, hop) for way in (0, 1) for hop in (1, 2, 3, 4)}

    def kv_hop(hop):
        for way in (0, 1):
            go(kv_copies[way, hop])

    def kv_wait(hop):
        for way in (0, 1):
            kv_copies[way, hop].wait_recv()

    piece = pl.ds(pl.multiple_of(core * PIECE, PIECE), PIECE)
    half = PIECE // 2
    low = pl.ds(pl.multiple_of(core * PIECE, half), half)
    high = pl.ds(pl.multiple_of(core * PIECE + half, half), half)
    others = [lax.rem(z + 1, GROUP), lax.rem(z + 3, GROUP), lax.rem(z + 2, GROUP)]

    def wz_copy(index, rows, step):
        return remote(
            w_ref.at[x, rows], wall.at[x, z, rows], wz_s.at[index], wz_r.at[index], at_zring(step)
        )

    wz_copies = [wz_copy(0, piece, 1), wz_copy(1, piece, -1), wz_copy(2, low, 2), wz_copy(3, high, -2)]

    def wx_copy(way, hop, sub):
        block = ring(x - hop + 1) if way == 0 else ring(x + hop - 1)
        rows = piece
        if hop == 4 and sub == 2:
            rows = low if way == 0 else high
        part = wall.at[block, others[sub], rows]
        return remote(part, part, wx_s.at[way, hop - 1, sub], wx_r.at[way, hop - 1, sub], at_x(1 if way == 0 else -1))

    wx_copies = {
        (way, hop, sub): wx_copy(way, hop, sub)
        for way in (0, 1) for hop in (1, 2, 3, 4) for sub in (0, 1, 2)
        if hop < 4 or sub == 2 or sub == way
    }

    def sib_copy(slot, sub):
        hop = (slot + 1) // 2
        block = ring(x - hop) if slot % 2 else ring(x + hop)
        part = wall.at[block, others[sub], piece]
        return remote(part, part, sib_s.at[slot, sub], sib_r.at[slot, sub], sibling)

    sib_copies = {(slot, sub): sib_copy(slot, sub) for slot in range(8) for sub in range(3)}

    def wx_first(sub):
        go(wx_copies[0, 1, sub])
        go(wx_copies[1, 1, sub])
        go(sib_copies[0, sub])

    def wx_pass(hop, sub):
        for way in (0, 1):
            wx_copies[way, hop, sub].wait_recv()
            if (way, hop + 1, sub) in wx_copies:
                go(wx_copies[way, hop + 1, sub])
            go(sib_copies[2 * hop - 1 + way, sub])

    def wx_last():
        for sub in (0, 1, 2):
            for way in (0, 1):
                if (way, 4, sub) in wx_copies:
                    wx_copies[way, 4, sub].wait_recv()
            go(sib_copies[7, sub])

    def sib_wait(slots):
        for slot in slots:
            for sub in range(3):
                sib_copies[slot, sub].wait_recv()

    def hid_copy(part):
        rows = pl.ds(part * 128, 128)
        return remote(hp_ref.at[rows], hbuf.at[rows], hid_s.at[part], hid_r.at[part], at_phase(1))

    hid_copies = [hid_copy(0), hid_copy(1)]

    def hid_start(part):
        @pl.when(p < 31)
        def _():
            hid_copies[part].start()

    def q_copy(step):
        there = ring(y + step)
        return remote(
            q_ref.at[:, pl.ds(pl.multiple_of(there * HEAD_DIM, HEAD_DIM), HEAD_DIM)],
            qbuf.at[y], q_s.at[step], q_r.at[step], at_y(step),
        )

    q_copies = [q_copy(step) for step in (4, 3, 5, 2, 6, 1, 7)]

    kv_hop(1)
    for copy in wz_copies:
        go(copy)
    for copy in q_copies:
        go(copy)

    acc[...] = jnp.zeros_like(acc)
    row_iota = lax.broadcasted_iota(jnp.int32, (BLOCK, BLOCK), 0)
    col_iota = lax.broadcasted_iota(jnp.int32, (BLOCK, BLOCK), 1)
    for qi in range(RING):
        seg_rows = jnp.broadcast_to(seg_ref[:, qi * BLOCK:(qi + 1) * BLOCK], (BLOCK, BLOCK)).T
        first = max(0, qi - 4)
        for kj in range(first, qi + 1):
            allowed = seg_rows == seg_ref[:, kj * BLOCK:(kj + 1) * BLOCK]
            if kj == qi:
                allowed = allowed & (col_iota <= row_iota)
            bias[qi, :, (kj - first) * BLOCK:(kj - first + 1) * BLOCK] = jnp.where(allowed, 0.0, MASKED)

    kv_wait(1)
    kv_hop(2)
    wz_copies[1].wait_recv()
    wx_first(0)
    wz_copies[0].wait_recv()
    wx_first(1)
    kv_wait(2)
    kv_hop(3)
    wz_copies[2].wait_recv()
    wz_copies[3].wait_recv()
    wx_first(2)
    hid_start(0)
    kv_wait(3)
    kv_hop(4)
    q_in.wait()
    for copy in q_copies:
        copy.wait_recv()
    kv_wait(4)
    wx_pass(1, 0)

    def attend(qi):
        first = max(0, qi - 4)
        count = (qi + 1 - first) * BLOCK
        keys = kv[first:qi + 1, 0].reshape(count, HEAD_DIM)
        vals = kv[first:qi + 1, 1].reshape(count, HEAD_DIM)
        scores = lax.dot_general(qbuf[qi], keys, (((1,), (1,)), ((), ())), preferred_element_type=F32)
        scores = scores * (HEAD_DIM ** -0.5 * LOG2_E) + bias[qi, :, :count]
        top = jnp.max(scores, axis=1, keepdims=True)
        probs = jnp.exp2(scores - top)
        total = jnp.sum(probs, axis=1, keepdims=True)
        heads_out = jnp.dot(probs.astype(BF16), vals, preferred_element_type=F32) / total
        astage[qi // 2, (qi % 2) * BLOCK:(qi % 2 + 1) * BLOCK, :] = heads_out.astype(BF16)

    own_copy = pltpu.make_async_copy(astage.at[z], aall.at[y, z], local_sem.at[5])

    def az_copy(b):
        return remote(astage.at[b], aall.at[y, z], az_s.at[b], az_r.at[z], at_z(b))

    for order, b in enumerate((3, 0, 2, 1)):
        attend(2 * b)
        attend(2 * b + 1)

        @pl.when(z == b)
        def _():
            own_copy.start()

        @pl.when(z != b)
        def _():
            az_copy(b).start()

        if order == 1:
            wx_pass(1, 1)

    def ay_copy(way, hop, sub):
        block = ring(y - hop + 1) if way == 0 else ring(y + hop - 1)
        part = aall.at[block, sources[sub]]
        return remote(part, part, ay_s.at[way, hop - 1, sub], ay_r.at[way, hop - 1, sub], at_y(1 if way == 0 else -1))

    upper = lax.div(z, 2)
    sources = [z, z + 1 - 2 * lax.rem(z, 2), 2 - upper, 3 - 3 * upper]
    ay_copies = {
        (way, hop, sub): ay_copy(way, hop, sub)
        for way in (0, 1) for hop in (1, 2, 3, 4) for sub in range(4)
        if hop < 4 or sub // 2 == way
    }

    def ay_first(sub):
        if sub == 0:
            own_copy.wait()
        else:
            remote(astage.at[0], aall.at[y, sources[sub]], az_s.at[0], az_r.at[sources[sub]], sibling).wait_recv()
        go(ay_copies[0, 1, sub])
        go(ay_copies[1, 1, sub])

    def ay_pass(hop, sub):
        for way in (0, 1):
            ay_copies[way, hop, sub].wait_recv()
            if (way, hop + 1, sub) in ay_copies:
                go(ay_copies[way, hop + 1, sub])

    def apart(there, here):
        ahead = lax.rem(there - here + RING, RING)
        return jnp.minimum(ahead, RING - ahead)

    def project(reach, before):
        def one(block, carry):
            far = jnp.maximum(apart(block, y), apart(block, x))

            @pl.when((far <= reach) & (far > before))
            def _():
                left = jnp.concatenate([aall[block, g] for g in range(GROUP)], axis=1)
                for tile in range(4):
                    cols = slice(tile * 256, (tile + 1) * 256)
                    right = wall[block, :, :, cols].reshape(GROUP * BLOCK, 256)
                    acc[:, cols] += jnp.dot(left, right, preferred_element_type=F32)

            return carry

        lax.fori_loop(0, RING, one, 0)

    ay_first(0)
    ay_first(1)
    ay_first(2)
    ay_first(3)
    hid_start(1)
    wx_pass(1, 2)
    ay_pass(1, 0)
    wx_pass(2, 0)
    ay_pass(1, 1)
    ay_pass(1, 2)
    wx_pass(2, 1)
    ay_pass(1, 3)
    ay_pass(2, 0)
    wx_pass(2, 2)
    ay_pass(2, 1)
    ay_pass(2, 2)
    wx_pass(3, 0)
    ay_pass(2, 3)
    w_in.wait()
    sib_wait((0, 1, 2, 3, 4))
    project(2, -1)
    ay_pass(3, 0)
    wx_pass(3, 1)
    ay_pass(3, 1)
    ay_pass(3, 2)
    wx_pass(3, 2)
    ay_pass(3, 3)
    wx_last()
    sib_wait((5, 6))
    project(3, 2)
    for sub in range(4):
        ay_copies[sub // 2, 4, sub].wait_recv()
    sib_wait((7,))
    project(4, 3)

    @pl.when(p == 0)
    def _():
        pltpu.make_async_copy(emb_ref, hbuf, local_sem.at[4]).wait()

    @pl.when(p > 0)
    def _():
        for copy in hid_copies:
            copy.wait_recv()

    out_ref[...] = (hbuf[...].astype(F32) + acc[...]).astype(BF16)

    for copy in sends:
        copy.wait_send()
    for b in range(GROUP):
        @pl.when(z != b)
        def _():
            az_copy(b).wait_send()

    @pl.when(p < 31)
    def _():
        for copy in hid_copies:
            copy.wait_send()


def on_device(queries, keys, values, seg_ids, out_weight, embedded, hidden_prev):
    rows, width = embedded.shape
    dma = pltpu.SemaphoreType.DMA
    hbm = pl.BlockSpec(memory_space=pl.ANY)
    vmem = pl.BlockSpec(memory_space=pltpu.VMEM)
    result = pl.pallas_call(
        kernel,
        out_shape=jax.ShapeDtypeStruct((rows, width), BF16),
        in_specs=[hbm, hbm, hbm, vmem, hbm, hbm, hbm],
        out_specs=vmem,
        scratch_shapes=[
            pltpu.VMEM((RING, BLOCK, HEAD_DIM), BF16),
            pltpu.VMEM((RING, 2, BLOCK, HEAD_DIM), BF16),
            pltpu.VMEM((RING, BLOCK, 5 * BLOCK), F32),
            pltpu.VMEM((GROUP, 2 * BLOCK, HEAD_DIM), BF16),
            pltpu.VMEM((RING, GROUP, 2 * BLOCK, HEAD_DIM), BF16),
            pltpu.VMEM((RING, GROUP, BLOCK, width), BF16),
            pltpu.VMEM((rows, width), BF16),
            pltpu.VMEM((rows, width), F32),
            dma((6,)),
            dma((2, 4)), dma((2, 4)),
            dma((8,)), dma((8,)),
            dma((4,)), dma((4,)),
            dma((2, 4, 3)), dma((2, 4, 3)),
            dma((8, 3)), dma((8, 3)),
            dma((2,)), dma((2,)),
            dma((4,)), dma((4,)),
            dma((2, 4, 4)), dma((2, 4, 4)),
        ],
        compiler_params=pltpu.CompilerParams(
            collective_id=0, has_side_effects=True, vmem_limit_bytes=48 * 1024 * 1024
        ),
    )(
        queries[0], keys[0], values[0], seg_ids,
        out_weight.reshape(RING, BLOCK, out_weight.shape[1]), embedded, hidden_prev[0],
    )
    return result[None]


def solution(mesh):
    return jax.shard_map(
        on_device,
        mesh=mesh,
        in_specs=(
            P("phase", "ctx", "tp"),
            P("phase", "ctx", "tp"),
            P("phase", "ctx", "tp"),
            P("phase", None),
            P("tp", "ctx"),
            P("tp", "ctx"),
            P("phase", "tp", "ctx"),
        ),
        out_specs=P("phase", "tp", "ctx"),
        check_vma=False,
    )
```

time: 176 us -> 78.8 us (0.45)
  the two profiles are of different devices: /device:TPU:14 before, /device:TPU:134 now
where the time goes in v1:
time: 78.8 us; the launch traced here: 78.3 us
  Pallas kernels  70.7 us (90%)
  local copies, waits for them, and re-layouts  7.62 us (10%)
    pallas_call x1, Pallas kernels, on_device(): pl.pallas_call(kernel, out_shape=jax.ShapeDtypeStruct((rows, width), BF16...  70.7 us
    unnamed x15, local copies, waits for them, and re-layouts  7.62 us

profile of v1, /device:TPU:134, one launch (start us, length us, event | category | flops | bytes accessed | tf_op | source)
XLA Modules:
  0.0 78.3 jit_solution(18035986194709948599)
XLA Ops:
  0.0 0.0 copy-start
  0.0 1.6 %copy-done = bf16[1024,1024]{1,0:T(8,128)(2,1)S(1)} copy-done((bf16[1024,1024]{1,0:T(8,128)(2,1)S(1)}, bf16[1024,1024]{1,0:T(8,128)(2,1)}, u32[]{:S(2)}) %copy-start) | copy-done | bytes 2097176
  1.6 0.0 copy-start.1
  1.6 1.0 %copy-done.1 = bf16[256,1024]{1,0:T(8,128)(2,1)S(1)} copy-done((bf16[256,1024]{1,0:T(8,128)(2,1)S(1)}, bf16[256,1024]{1,0:T(8,128)(2,1)}, u32[]{:S(2)}) %copy-start.1) | copy-done | bytes 524312
  2.6 0.0 copy-start.2
  2.6 1.0 %copy-done.2 = bf16[1,256,1024]{2,1,0:T(8,128)(2,1)S(1)} copy-done((bf16[1,256,1024]{2,1,0:T(8,128)(2,1)S(1)}, bf16[1,256,1024]{2,1,0:T(8,128)(2,1)}, u32[]{:S(2)}) %copy-start.2) | copy-done | bytes 524312
  3.7 0.0 copy-start.3
  3.7 0.9 %copy-done.3 = bf16[1,128,1024]{2,1,0:T(8,128)(2,1)S(1)} copy-done((bf16[1,128,1024]{2,1,0:T(8,128)(2,1)S(1)}, bf16[1,128,1024]{2,1,0:T(8,128)(2,1)}, u32[]{:S(2)}) %copy-start.3) | copy-done | bytes 262168
  4.6 0.0 copy-start.4
  4.6 0.8 copy-done.4
  5.4 0.0 copy-start.5
  5.4 0.8 copy-done.5
  6.1 0.0 copy-start.6
  6.1 0.7 copy-done.6
  6.8 70.7 %shard_map.73 = bf16[256,1024]{1,0:T(8,128)(2,1)S(1)} custom-call(bf16[128,1024]{1,0:T(8,128)(2,1)S(1)} %bitcast.9, bf16[128,128]{1,0:T(8,128)(2,1)S(1)} %bitcast.10, bf16[128,128]{1,0:T(8,128)(2,1)S(1)} %bitcast.11, s32[1,1024]{1,0:T(1,128)S(1)} %copy-done.6, bf16[8,128,1024]{2,1,0:T(8,128)(2,1)S(1)} %bitcast.6, bf16[256,1024]{1,0:T(8,128)(2,1)S(1)} %copy-done.1, ...), custom_call_target="tpu_custom_call" | custom-call | tf_op jit(solution)/shard_map/pallas_call | solution.py:368
  77.5 0.8 %copy.9 = bf16[1,256,1024]{2,1,0:T(8,128)(2,1)} copy(bf16[1,256,1024]{2,1,0:T(8,128)(2,1)S(1)} %bitcast.7) | data formatting | bytes 1048576
Async XLA Ops:
  0.0 1.6 %copy-start = (bf16[1024,1024]{1,0:T(8,128)(2,1)S(1)}, bf16[1024,1024]{1,0:T(8,128)(2,1)}, u32[]{:S(2)}) copy-start(bf16[1024,1024]{1,0:T(8,128)(2,1)} %param.11) | copy-start | bytes 6291460
  1.6 1.0 %copy-start.1 = (bf16[256,1024]{1,0:T(8,128)(2,1)S(1)}, bf16[256,1024]{1,0:T(8,128)(2,1)}, u32[]{:S(2)}) copy-start(bf16[256,1024]{1,0:T(8,128)(2,1)} %emb_ref.1) | copy-start | bytes 1572868
  2.6 1.0 %copy-start.2 = (bf16[1,256,1024]{2,1,0:T(8,128)(2,1)S(1)}, bf16[1,256,1024]{2,1,0:T(8,128)(2,1)}, u32[]{:S(2)}) copy-start(bf16[1,256,1024]{2,1,0:T(8,128)(2,1)} %param.13) | copy-start | bytes 1572868
  3.7 0.9 %copy-start.3 = (bf16[1,128,1024]{2,1,0:T(8,128)(2,1)S(1)}, bf16[1,128,1024]{2,1,0:T(8,128)(2,1)}, u32[]{:S(2)}) copy-start(bf16[1,128,1024]{2,1,0:T(8,128)(2,1)} %param.7) | copy-start | bytes 786436
  4.6 0.8 copy-start.4
  5.4 0.8 copy-start.5
  6.1 0.7 copy-start.6

commit v2 on v1

--- a/solution.py
+++ b/solution.py
@@ -17,9 +17,9 @@
 
 
 def kernel(
-    q_ref, k_ref, v_ref, seg_ref, w_ref, emb_ref, hp_ref, out_ref,
-    qbuf, kv, bias, astage, aall, wall, hbuf, acc,
-    local_sem, kv_s, kv_r, q_s, q_r, wz_s, wz_r, wx_s, wx_r, sib_s, sib_r, hid_s, hid_r, az_s, az_r, ay_s, ay_r,
+    q_ref, k_ref, v_ref, seg_in, w_ref, emb_ref, hp_ref, out_ref,
+    seg, qbuf, kv, bias, astage, aall, wall, hbuf, acc,
+    ready, hid_ready, local_sem, kv_s, kv_r, q_s, q_r, wz_s, wz_r, wx_s, wx_r, sib_s, sib_r, hid_s, hid_r, az_s, az_r, ay_s, ay_r,
 ):
     p = lax.axis_index("phase")
     y = lax.axis_index("ctx")
@@ -27,7 +27,6 @@
     x = lax.div(p, 4)
     zh = lax.rem(lax.div(p, 2), 2)
     core = lax.rem(p, 2)
-    zring = zh * GROUP + z
 
     def ring(value):
         return lax.rem(value + 2 * RING, RING)
@@ -37,10 +36,6 @@
 
     def at_x(step):
         return {"phase": lax.rem(p + 4 * step + 32, 32), "ctx": y, "tp": z}
-
-    def at_zring(step):
-        there = ring(zring + step)
-        return {"phase": x * 4 + lax.div(there, GROUP) * 2 + core, "ctx": y, "tp": lax.rem(there, GROUP)}
 
     def at_z(place):
         return {"phase": p, "ctx": y, "tp": place}
@@ -56,13 +51,21 @@
             device_id=where, device_id_type=pl.DeviceIdType.MESH,
         )
 
+    def signal(sem, where):
+        pl.semaphore_signal(sem, inc=1, device_id=where, device_id_type=pl.DeviceIdType.MESH)
+
     barrier = pltpu.get_barrier_semaphore()
-    greeted = [at_y(d) for d in range(1, RING)]
-    greeted += [at_z(lax.rem(z + d, GROUP)) for d in range(1, GROUP)]
-    greeted += [at_zring(d) for d in (1, -1, 2, -2)]
-    greeted += [at_x(1), at_x(-1), sibling, at_phase(1), at_phase(-1)]
+    greeted = [at_y(d) for d in range(1, RING)] + [at_x(1), at_x(-1), sibling]
     for peer in greeted:
-        pl.semaphore_signal(barrier, inc=1, device_id=peer, device_id_type=pl.DeviceIdType.MESH)
+        signal(barrier, peer)
+    for d in range(1, GROUP):
+        @pl.when(z + d < GROUP)
+        def _():
+            signal(barrier, at_z(z + d))
+
+    @pl.when(zh == 0)
+    def _():
+        signal(barrier, at_phase(2 * core - 1))
 
     k_in = pltpu.make_async_copy(k_ref, kv.at[y, 0], local_sem.at[0])
     v_in = pltpu.make_async_copy(v_ref, kv.at[y, 1], local_sem.at[1])
@@ -73,6 +76,8 @@
     k_in.start()
     v_in.start()
     q_in.start()
+    seg_copy = pltpu.make_async_copy(seg_in, seg, local_sem.at[6])
+    seg_copy.start()
     w_in.start()
 
     @pl.when(p == 0)
@@ -81,7 +86,15 @@
 
     k_in.wait()
     v_in.wait()
-    pl.semaphore_wait(barrier, len(greeted))
+    pl.semaphore_wait(barrier, len(greeted) + z + zh)
+    for d in range(1, GROUP):
+        @pl.when(z - d >= 0)
+        def _():
+            signal(ready.at[z], at_z(z - d))
+
+    @pl.when((zh == 1) & (core == 0))
+    def _():
+        signal(hid_ready, at_phase(-1))
 
     sends = []
 
@@ -89,33 +102,54 @@
         copy.start()
         sends.append(copy)
 
-    def kv_copy(way, hop):
+    def kv_copy(way, hop, part):
         block = ring(y - hop + 1) if way == 0 else ring(y + hop - 1)
-        part = kv.at[block] if hop < 4 else kv.at[block, way]
-        return remote(part, part, kv_s.at[way, hop - 1], kv_r.at[way, hop - 1], at_y(1 if way == 0 else -1))
-
-    kv_copies = {(way, hop): kv_copy(way, hop) for way in (0, 1) for hop in (1, 2, 3, 4)}
-
-    def kv_hop(hop):
-        for way in (0, 1):
-            go(kv_copies[way, hop])
-
-    def kv_wait(hop):
-        for way in (0, 1):
-            kv_copies[way, hop].wait_recv()
+        held = kv.at[block, part]
+        return remote(
+            held, held, kv_s.at[way, hop - 1, part], kv_r.at[way, hop - 1, part], at_y(1 if way == 0 else -1)
+        )
+
+    kv_copies = {
+        (way, hop, part): kv_copy(way, hop, part)
+        for way in (0, 1) for hop in (1, 2, 3, 4) for part in (0, 1)
+        if hop < 4 or part == way
+    }
+
+    def kv_pass(hop):
+        for part in (0, 1):
+            for way in (0, 1):
+                if (way, hop, part) in kv_copies:
+                    kv_copies[way, hop, part].wait_recv()
+                if (way, hop + 1, part) in kv_copies:
+                    go(kv_copies[way, hop + 1, part])
 
     piece = pl.ds(pl.multiple_of(core * PIECE, PIECE), PIECE)
     half = PIECE // 2
     low = pl.ds(pl.multiple_of(core * PIECE, half), half)
     high = pl.ds(pl.multiple_of(core * PIECE + half, half), half)
-    others = [lax.rem(z + 1, GROUP), lax.rem(z + 3, GROUP), lax.rem(z + 2, GROUP)]
-
-    def wz_copy(index, rows, step):
-        return remote(
-            w_ref.at[x, rows], wall.at[x, z, rows], wz_s.at[index], wz_r.at[index], at_zring(step)
-        )
-
-    wz_copies = [wz_copy(0, piece, 1), wz_copy(1, piece, -1), wz_copy(2, low, 2), wz_copy(3, high, -2)]
+    first = jnp.abs(z - 1)
+    last = 3 - 3 * lax.div(z, 3)
+    others = [first, 6 - z - first - last, last]
+    sources = [z] + others
+
+    def wz_copy(there):
+        return remote(w_ref.at[x, piece], wall.at[x, z, piece], wz_s.at[there], wz_r.at[z], at_z(there))
+
+    def wz_down():
+        for d in range(1, GROUP):
+            @pl.when(z - d >= 0)
+            def _():
+                wz_copy(z - d).start()
+
+    def wz_up(d):
+        @pl.when(z + d < GROUP)
+        def _():
+            pl.semaphore_wait(ready.at[z + d], 1)
+            wz_copy(z + d).start()
+
+    def wz_wait(sub):
+        held = wall.at[x, others[sub], piece]
+        remote(held, held, wz_s.at[others[sub]], wz_r.at[others[sub]], sibling).wait_recv()
 
     def wx_copy(way, hop, sub):
         block = ring(x - hop + 1) if way == 0 else ring(x + hop - 1)
@@ -170,6 +204,11 @@
     hid_copies = [hid_copy(0), hid_copy(1)]
 
     def hid_start(part):
+        if part == 0:
+            @pl.when((zh == 0) & (core == 1))
+            def _():
+                pl.semaphore_wait(hid_ready, 1)
+
         @pl.when(p < 31)
         def _():
             hid_copies[part].start()
@@ -181,51 +220,54 @@
             qbuf.at[y], q_s.at[step], q_r.at[step], at_y(step),
         )
 
-    q_copies = [q_copy(step) for step in (4, 3, 5, 2, 6, 1, 7)]
-
-    kv_hop(1)
-    for copy in wz_copies:
-        go(copy)
-    for copy in q_copies:
-        go(copy)
+    q_copies = {step: q_copy(step) for step in range(1, RING)}
+
+    for part in (0, 1):
+        for way in (0, 1):
+            go(kv_copies[way, 1, part])
+    wz_down()
+    go(q_copies[4])
 
     acc[...] = jnp.zeros_like(acc)
+    seg_copy.wait()
     row_iota = lax.broadcasted_iota(jnp.int32, (BLOCK, BLOCK), 0)
     col_iota = lax.broadcasted_iota(jnp.int32, (BLOCK, BLOCK), 1)
     for qi in range(RING):
-        seg_rows = jnp.broadcast_to(seg_ref[:, qi * BLOCK:(qi + 1) * BLOCK], (BLOCK, BLOCK)).T
-        first = max(0, qi - 4)
-        for kj in range(first, qi + 1):
-            allowed = seg_rows == seg_ref[:, kj * BLOCK:(kj + 1) * BLOCK]
+        seg_rows = jnp.broadcast_to(seg[:, qi * BLOCK:(qi + 1) * BLOCK], (BLOCK, BLOCK)).T
+        low_key = max(0, qi - 4)
+        for kj in range(low_key, qi + 1):
+            allowed = seg_rows == seg[:, kj * BLOCK:(kj + 1) * BLOCK]
             if kj == qi:
                 allowed = allowed & (col_iota <= row_iota)
-            bias[qi, :, (kj - first) * BLOCK:(kj - first + 1) * BLOCK] = jnp.where(allowed, 0.0, MASKED)
-
-    kv_wait(1)
-    kv_hop(2)
-    wz_copies[1].wait_recv()
+            bias[qi, :, (kj - low_key) * BLOCK:(kj - low_key + 1) * BLOCK] = jnp.where(allowed, 0.0, MASKED)
+
+    kv_pass(1)
+    go(q_copies[3])
+    go(q_copies[5])
+    kv_pass(2)
+    go(q_copies[2])
+    go(q_copies[6])
+    wz_up(1)
+    kv_pass(3)
+    go(q_copies[1])
+    go(q_copies[7])
+    wz_up(2)
+    wz_wait(0)
     wx_first(0)
-    wz_copies[0].wait_recv()
+    q_in.wait()
+    for copy in q_copies.values():
+        copy.wait_recv()
+    kv_pass(4)
+    wz_up(3)
+    wz_wait(1)
     wx_first(1)
-    kv_wait(2)
-    kv_hop(3)
-    wz_copies[2].wait_recv()
-    wz_copies[3].wait_recv()
-    wx_first(2)
     hid_start(0)
-    kv_wait(3)
-    kv_hop(4)
-    q_in.wait()
-    for copy in q_copies:
-        copy.wait_recv()
-    kv_wait(4)
-    wx_pass(1, 0)
 
     def attend(qi):
-        first = max(0, qi - 4)
-        count = (qi + 1 - first) * BLOCK
-        keys = kv[first:qi + 1, 0].reshape(count, HEAD_DIM)
-        vals = kv[first:qi + 1, 1].reshape(count, HEAD_DIM)
+        low_key = max(0, qi - 4)
+        count = (qi + 1 - low_key) * BLOCK
+        keys = kv[low_key:qi + 1, 0].reshape(count, HEAD_DIM)
+        vals = kv[low_key:qi + 1, 1].reshape(count, HEAD_DIM)
         scores = lax.dot_general(qbuf[qi], keys, (((1,), (1,)), ((), ())), preferred_element_type=F32)
         scores = scores * (HEAD_DIM ** -0.5 * LOG2_E) + bias[qi, :, :count]
         top = jnp.max(scores, axis=1, keepdims=True)
@@ -239,7 +281,7 @@
     def az_copy(b):
         return remote(astage.at[b], aall.at[y, z], az_s.at[b], az_r.at[z], at_z(b))
 
-    for order, b in enumerate((3, 0, 2, 1)):
+    for b in range(GROUP):
         attend(2 * b)
         attend(2 * b + 1)
 
@@ -251,7 +293,12 @@
         def _():
             az_copy(b).start()
 
-        if order == 1:
+        if b == 0:
+            wx_pass(1, 0)
+        if b == 1:
+            wz_wait(2)
+            wx_first(2)
+        if b == 3:
             wx_pass(1, 1)
 
     def ay_copy(way, hop, sub):
@@ -259,8 +306,6 @@
         part = aall.at[block, sources[sub]]
         return remote(part, part, ay_s.at[way, hop - 1, sub], ay_r.at[way, hop - 1, sub], at_y(1 if way == 0 else -1))
 
-    upper = lax.div(z, 2)
-    sources = [z, z + 1 - 2 * lax.rem(z, 2), 2 - upper, 3 - 3 * upper]
     ay_copies = {
         (way, hop, sub): ay_copy(way, hop, sub)
         for way in (0, 1) for hop in (1, 2, 3, 4) for sub in range(4)
@@ -302,28 +347,28 @@
         lax.fori_loop(0, RING, one, 0)
 
     ay_first(0)
+    wx_pass(1, 2)
     ay_first(1)
+    wx_pass(2, 0)
+    ay_pass(1, 0)
     ay_first(2)
+    wx_pass(2, 1)
+    ay_pass(1, 1)
     ay_first(3)
     hid_start(1)
-    wx_pass(1, 2)
-    ay_pass(1, 0)
-    wx_pass(2, 0)
-    ay_pass(1, 1)
     ay_pass(1, 2)
-    wx_pass(2, 1)
+    wx_pass(2, 2)
+    ay_pass(2, 0)
     ay_pass(1, 3)
-    ay_pass(2, 0)
-    wx_pass(2, 2)
+    wx_pass(3, 0)
     ay_pass(2, 1)
     ay_pass(2, 2)
-    wx_pass(3, 0)
+    wx_pass(3, 1)
+    ay_pass(3, 0)
     ay_pass(2, 3)
     w_in.wait()
     sib_wait((0, 1, 2, 3, 4))
     project(2, -1)
-    ay_pass(3, 0)
-    wx_pass(3, 1)
     ay_pass(3, 1)
     ay_pass(3, 2)
     wx_pass(3, 2)
@@ -353,6 +398,7 @@
         @pl.when(z != b)
         def _():
             az_copy(b).wait_send()
+            wz_copy(b).wait_send()
 
     @pl.when(p < 31)
     def _():
@@ -363,14 +409,19 @@
 def on_device(queries, keys, values, seg_ids, out_weight, embedded, hidden_prev):
     rows, width = embedded.shape
     dma = pltpu.SemaphoreType.DMA
-    hbm = pl.BlockSpec(memory_space=pl.ANY)
+    hbm = pl.BlockSpec(memory_space=pltpu.HBM)
     vmem = pl.BlockSpec(memory_space=pltpu.VMEM)
+    operands = (
+        queries[0], keys[0], values[0], seg_ids,
+        out_weight.reshape(RING, BLOCK, out_weight.shape[1]), embedded, hidden_prev[0],
+    )
     result = pl.pallas_call(
         kernel,
         out_shape=jax.ShapeDtypeStruct((rows, width), BF16),
-        in_specs=[hbm, hbm, hbm, vmem, hbm, hbm, hbm],
+        in_specs=[hbm] * 7,
         out_specs=vmem,
         scratch_shapes=[
+            pltpu.VMEM((1, RING * BLOCK), jnp.int32),
             pltpu.VMEM((RING, BLOCK, HEAD_DIM), BF16),
             pltpu.VMEM((RING, 2, BLOCK, HEAD_DIM), BF16),
             pltpu.VMEM((RING, BLOCK, 5 * BLOCK), F32),
@@ -379,8 +430,9 @@
             pltpu.VMEM((RING, GROUP, BLOCK, width), BF16),
             pltpu.VMEM((rows, width), BF16),
             pltpu.VMEM((rows, width), F32),
-            dma((6,)),
-            dma((2, 4)), dma((2, 4)),
+            pltpu.SemaphoreType.REGULAR((GROUP,)), pltpu.SemaphoreType.REGULAR,
+            dma((7,)),
+            dma((2, 4, 2)), dma((2, 4, 2)),
             dma((8,)), dma((8,)),
             dma((4,)), dma((4,)),
             dma((2, 4, 3)), dma((2, 4, 3)),
@@ -392,10 +444,7 @@
         compiler_params=pltpu.CompilerParams(
             collective_id=0, has_side_effects=True, vmem_limit_bytes=48 * 1024 * 1024
         ),
-    )(
-        queries[0], keys[0], values[0], seg_ids,
-        out_weight.reshape(RING, BLOCK, out_weight.shape[1]), embedded, hidden_prev[0],
-    )
+    )(*(pltpu.with_memory_space_constraint(operand, pltpu.HBM) for operand in operands))
     return result[None]
 
 

time: 78.8 us -> 77.3 us (0.981)
  the two profiles are of different devices: /device:TPU:134 before, /device:TPU:899 now
where the time goes in v2:
time: 77.3 us; the launch traced here: 77.2 us
  Pallas kernels  76.4 us (99%)
  local copies, waits for them, and re-layouts  0.8 us (1%)
    pallas_call x1, Pallas kernels, on_device(): pl.pallas_call(kernel, out_shape=jax.ShapeDtypeStruct((rows, width), BF16...  76.4 us

profile of v2, /device:TPU:899, one launch (start us, length us, event | category | flops | bytes accessed | tf_op | source)
XLA Modules:
  0.0 77.2 jit_solution(4737376401453437588)
XLA Ops:
  0.0 76.4 %shard_map.73 = bf16[256,1024]{1,0:T(8,128)(2,1)S(1)} custom-call(bf16[128,1024]{1,0:T(8,128)(2,1)} %bitcast.9, bf16[128,128]{1,0:T(8,128)(2,1)} %bitcast.10, bf16[128,128]{1,0:T(8,128)(2,1)} %bitcast.11, s32[1,1024]{1,0:T(1,128)} %seg_in.1, bf16[8,128,1024]{2,1,0:T(8,128)(2,1)} %bitcast.7, bf16[256,1024]{1,0:T(8,128)(2,1)} %emb_ref.1, bf16[256,1024]{1,0:T(8,128)(2,1)} %bitcast.8), custom_call_target="tpu_custom_call" | custom-call | tf_op jit(solution)/shard_map/pallas_call | solution.py:418
  76.4 0.8 %copy.9 = bf16[1,256,1024]{2,1,0:T(8,128)(2,1)} copy(bf16[1,256,1024]{2,1,0:T(8,128)(2,1)S(1)} %bitcast.6) | data formatting | bytes 1048576

commit v3 on v2

--- a/solution.py
+++ b/solution.py
@@ -55,7 +55,7 @@
         pl.semaphore_signal(sem, inc=1, device_id=where, device_id_type=pl.DeviceIdType.MESH)
 
     barrier = pltpu.get_barrier_semaphore()
-    greeted = [at_y(d) for d in range(1, RING)] + [at_x(1), at_x(-1), sibling]
+    greeted = [at_y(1), at_y(-1), at_x(1), at_x(-1), sibling]
     for peer in greeted:
         signal(barrier, peer)
     for d in range(1, GROUP):
@@ -84,8 +84,6 @@
     def _():
         pltpu.make_async_copy(emb_ref, hbuf, local_sem.at[4]).start()
 
-    k_in.wait()
-    v_in.wait()
     pl.semaphore_wait(barrier, len(greeted) + z + zh)
     for d in range(1, GROUP):
         @pl.when(z - d >= 0)
@@ -106,7 +104,7 @@
         block = ring(y - hop + 1) if way == 0 else ring(y + hop - 1)
         held = kv.at[block, part]
         return remote(
-            held, held, kv_s.at[way, hop - 1, part], kv_r.at[way, hop - 1, part], at_y(1 if way == 0 else -1)
+            held if hop > 1 else (k_ref, v_ref)[part], held, kv_s.at[way, hop - 1, part], kv_r.at[way, hop - 1, part], at_y(1 if way == 0 else -1)
         )
 
     kv_copies = {
@@ -198,20 +196,20 @@
                 sib_copies[slot, sub].wait_recv()
 
     def hid_copy(part):
-        rows = pl.ds(part * 128, 128)
+        rows = pl.ds(part * PIECE, PIECE)
         return remote(hp_ref.at[rows], hbuf.at[rows], hid_s.at[part], hid_r.at[part], at_phase(1))
 
-    hid_copies = [hid_copy(0), hid_copy(1)]
-
-    def hid_start(part):
-        if part == 0:
-            @pl.when((zh == 0) & (core == 1))
-            def _():
-                pl.semaphore_wait(hid_ready, 1)
+    hid_copies = [hid_copy(part) for part in range(4)]
+
+    def hid_start():
+        @pl.when((zh == 0) & (core == 1))
+        def _():
+            pl.semaphore_wait(hid_ready, 1)
 
         @pl.when(p < 31)
         def _():
-            hid_copies[part].start()
+            for copy in hid_copies:
+                copy.start()
 
     def q_copy(step):
         there = ring(y + step)
@@ -226,7 +224,8 @@
         for way in (0, 1):
             go(kv_copies[way, 1, part])
     wz_down()
-    go(q_copies[4])
+    go(q_copies[1])
+    go(q_copies[7])
 
     acc[...] = jnp.zeros_like(acc)
     seg_copy.wait()
@@ -242,26 +241,29 @@
             bias[qi, :, (kj - low_key) * BLOCK:(kj - low_key + 1) * BLOCK] = jnp.where(allowed, 0.0, MASKED)
 
     kv_pass(1)
-    go(q_copies[3])
-    go(q_copies[5])
-    kv_pass(2)
     go(q_copies[2])
     go(q_copies[6])
     wz_up(1)
-    kv_pass(3)
-    go(q_copies[1])
-    go(q_copies[7])
-    wz_up(2)
+    kv_pass(2)
+    go(q_copies[3])
+    go(q_copies[5])
     wz_wait(0)
     wx_first(0)
+    wz_up(2)
+    kv_pass(3)
+    go(q_copies[4])
+    wz_wait(1)
+    wx_first(1)
+    wz_up(3)
+    kv_pass(4)
+    wx_pass(1, 0)
+    wz_wait(2)
+    wx_first(2)
+    k_in.wait()
+    v_in.wait()
     q_in.wait()
     for copy in q_copies.values():
         copy.wait_recv()
-    kv_pass(4)
-    wz_up(3)
-    wz_wait(1)
-    wx_first(1)
-    hid_start(0)
 
     def attend(qi):
         low_key = max(0, qi - 4)
@@ -293,12 +295,7 @@
         def _():
             az_copy(b).start()
 
-        if b == 0:
-            wx_pass(1, 0)
         if b == 1:
-            wz_wait(2)
-            wx_first(2)
-        if b == 3:
             wx_pass(1, 1)
 
     def ay_copy(way, hop, sub):
@@ -347,31 +344,31 @@
         lax.fori_loop(0, RING, one, 0)
 
     ay_first(0)
+    wx_pass(2, 0)
     wx_pass(1, 2)
     ay_first(1)
-    wx_pass(2, 0)
     ay_pass(1, 0)
+    wx_pass(2, 1)
     ay_first(2)
-    wx_pass(2, 1)
     ay_pass(1, 1)
+    wx_pass(3, 0)
+    ay_pass(2, 0)
+    wx_pass(2, 2)
+    ay_pass(1, 2)
     ay_first(3)
-    hid_start(1)
-    ay_pass(1, 2)
-    wx_pass(2, 2)
-    ay_pass(2, 0)
+    hid_start()
+    ay_pass(2, 1)
+    wx_pass(3, 1)
+    ay_pass(2, 2)
+    ay_pass(3, 0)
     ay_pass(1, 3)
-    wx_pass(3, 0)
-    ay_pass(2, 1)
-    ay_pass(2, 2)
-    wx_pass(3, 1)
-    ay_pass(3, 0)
+    wx_pass(3, 2)
+    ay_pass(3, 1)
     ay_pass(2, 3)
     w_in.wait()
     sib_wait((0, 1, 2, 3, 4))
     project(2, -1)
-    ay_pass(3, 1)
     ay_pass(3, 2)
-    wx_pass(3, 2)
     ay_pass(3, 3)
     wx_last()
     sib_wait((5, 6))
@@ -437,7 +434,7 @@
             dma((4,)), dma((4,)),
             dma((2, 4, 3)), dma((2, 4, 3)),
             dma((8, 3)), dma((8, 3)),
-            dma((2,)), dma((2,)),
+            dma((4,)), dma((4,)),
             dma((4,)), dma((4,)),
             dma((2, 4, 4)), dma((2, 4, 4)),
         ],

time: 77.3 us -> 68 us (0.88)
  the two profiles are of different devices: /device:TPU:899 before, /device:TPU:14 now
where the time goes in v3:
time: 68 us; the launch traced here: 66.9 us
  Pallas kernels  66.1 us (97%)
  local copies, waits for them, and re-layouts  0.8 us (1%)
    pallas_call x1, Pallas kernels, on_device(): pl.pallas_call(kernel, out_shape=jax.ShapeDtypeStruct((rows, width), BF16...  66.1 us

profile of v3, /device:TPU:14, one launch (start us, length us, event | category | flops | bytes accessed | tf_op | source)
XLA Modules:
  0.0 66.9 jit_solution(4762394872880560166)
XLA Ops:
  0.0 66.1 %shard_map.73 = bf16[256,1024]{1,0:T(8,128)(2,1)S(1)} custom-call(bf16[128,1024]{1,0:T(8,128)(2,1)} %bitcast.9, bf16[128,128]{1,0:T(8,128)(2,1)} %bitcast.10, bf16[128,128]{1,0:T(8,128)(2,1)} %bitcast.11, s32[1,1024]{1,0:T(1,128)} %seg_in.1, bf16[8,128,1024]{2,1,0:T(8,128)(2,1)} %bitcast.7, bf16[256,1024]{1,0:T(8,128)(2,1)} %emb_ref.1, bf16[256,1024]{1,0:T(8,128)(2,1)} %bitcast.8), custom_call_target="tpu_custom_call" | custom-call | tf_op jit(solution)/shard_map/pallas_call | solution.py:415
  66.1 0.8 %copy.9 = bf16[1,256,1024]{2,1,0:T(8,128)(2,1)} copy(bf16[1,256,1024]{2,1,0:T(8,128)(2,1)S(1)} %bitcast.6) | data formatting | bytes 1048576

commit v4 on v3

--- a/solution.py
+++ b/solution.py
@@ -19,7 +19,7 @@
 def kernel(
     q_ref, k_ref, v_ref, seg_in, w_ref, emb_ref, hp_ref, out_ref,
     seg, qbuf, kv, bias, astage, aall, wall, hbuf, acc,
-    ready, hid_ready, local_sem, kv_s, kv_r, q_s, q_r, wz_s, wz_r, wx_s, wx_r, sib_s, sib_r, hid_s, hid_r, az_s, az_r, ay_s, ay_r,
+    ready, hid_ready, x_ready, sib_ready, local_sem, kv_s, kv_r, q_s, q_r, wz_s, wz_r, wx_s, wx_r, sib_s, sib_r, hid_s, hid_r, az_s, az_r, ay_s, ay_r,
 ):
     p = lax.axis_index("phase")
     y = lax.axis_index("ctx")
@@ -55,9 +55,21 @@
         pl.semaphore_signal(sem, inc=1, device_id=where, device_id_type=pl.DeviceIdType.MESH)
 
     barrier = pltpu.get_barrier_semaphore()
-    greeted = [at_y(1), at_y(-1), at_x(1), at_x(-1), sibling]
-    for peer in greeted:
+    lane = y + z + zh + core
+    tail = (lane == 0) & (x == 0)
+    beside = (lane == 0) & ((x == 1) | (x == RING - 1))
+    for peer in (at_y(1), at_y(-1)):
         signal(barrier, peer)
+
+    @pl.when(jnp.logical_not(tail))
+    def _():
+        for peer in (at_x(1), at_x(-1)):
+            signal(barrier, peer)
+
+    @pl.when(core == 1)
+    def _():
+        signal(barrier, sibling)
+
     for d in range(1, GROUP):
         @pl.when(z + d < GROUP)
         def _():
@@ -84,7 +96,18 @@
     def _():
         pltpu.make_async_copy(emb_ref, hbuf, local_sem.at[4]).start()
 
-    pl.semaphore_wait(barrier, len(greeted) + z + zh)
+    awaited = 5 - core + z + zh - jnp.where(beside, 1, 0)
+    pl.semaphore_wait(barrier, awaited)
+
+    @pl.when(tail)
+    def _():
+        for peer in (at_x(1), at_x(-1)):
+            signal(x_ready, peer)
+
+    @pl.when(core == 0)
+    def _():
+        signal(sib_ready, sibling)
+
     for d in range(1, GROUP):
         @pl.when(z - d >= 0)
         def _():
@@ -248,6 +271,15 @@
     go(q_copies[3])
     go(q_copies[5])
     wz_wait(0)
+
+    @pl.when(beside)
+    def _():
+        pl.semaphore_wait(x_ready, 1)
+
+    @pl.when(core == 1)
+    def _():
+        pl.semaphore_wait(sib_ready, 1)
+
     wx_first(0)
     wz_up(2)
     kv_pass(3)
@@ -344,32 +376,32 @@
         lax.fori_loop(0, RING, one, 0)
 
     ay_first(0)
-    wx_pass(2, 0)
     wx_pass(1, 2)
     ay_first(1)
     ay_pass(1, 0)
-    wx_pass(2, 1)
+    wx_pass(2, 0)
     ay_first(2)
     ay_pass(1, 1)
-    wx_pass(3, 0)
+    wx_pass(2, 1)
     ay_pass(2, 0)
+    ay_pass(1, 2)
     wx_pass(2, 2)
-    ay_pass(1, 2)
     ay_first(3)
     hid_start()
     ay_pass(2, 1)
-    wx_pass(3, 1)
+    wx_pass(3, 0)
     ay_pass(2, 2)
     ay_pass(3, 0)
     ay_pass(1, 3)
-    wx_pass(3, 2)
+    wx_pass(3, 1)
     ay_pass(3, 1)
     ay_pass(2, 3)
+    wx_pass(3, 2)
+    ay_pass(3, 2)
+    ay_pass(3, 3)
     w_in.wait()
     sib_wait((0, 1, 2, 3, 4))
     project(2, -1)
-    ay_pass(3, 2)
-    ay_pass(3, 3)
     wx_last()
     sib_wait((5, 6))
     project(3, 2)
@@ -428,6 +460,7 @@
             pltpu.VMEM((rows, width), BF16),
             pltpu.VMEM((rows, width), F32),
             pltpu.SemaphoreType.REGULAR((GROUP,)), pltpu.SemaphoreType.REGULAR,
+            pltpu.SemaphoreType.REGULAR, pltpu.SemaphoreType.REGULAR,
             dma((7,)),
             dma((2, 4, 2)), dma((2, 4, 2)),
             dma((8,)), dma((8,)),

time: 68 us -> 65.4 us (0.962)
  the two profiles are of different devices: /device:TPU:14 before, /device:TPU:2 now
where the time goes in v4:
time: 65.4 us; the launch traced here: 65.2 us
  Pallas kernels  64.4 us (98%)
  local copies, waits for them, and re-layouts  0.8 us (1%)
    pallas_call x1, Pallas kernels, on_device(): pl.pallas_call(kernel, out_shape=jax.ShapeDtypeStruct((rows, width), BF16...  64.4 us

profile of v4, /device:TPU:2, one launch (start us, length us, event | category | flops | bytes accessed | tf_op | source)
XLA Modules:
  0.0 65.2 jit_solution(16753364289336335860)
XLA Ops:
  0.0 64.4 %shard_map.73 = bf16[256,1024]{1,0:T(8,128)(2,1)S(1)} custom-call(bf16[128,1024]{1,0:T(8,128)(2,1)} %bitcast.9, bf16[128,128]{1,0:T(8,128)(2,1)} %bitcast.10, bf16[128,128]{1,0:T(8,128)(2,1)} %bitcast.11, s32[1,1024]{1,0:T(1,128)} %seg_in.1, bf16[8,128,1024]{2,1,0:T(8,128)(2,1)} %bitcast.7, bf16[256,1024]{1,0:T(8,128)(2,1)} %emb_ref.1, bf16[256,1024]{1,0:T(8,128)(2,1)} %bitcast.8), custom_call_target="tpu_custom_call" | custom-call | tf_op jit(solution)/shard_map/pallas_call | solution.py:447
  64.4 0.8 %copy.9 = bf16[1,256,1024]{2,1,0:T(8,128)(2,1)} copy(bf16[1,256,1024]{2,1,0:T(8,128)(2,1)S(1)} %bitcast.6) | data formatting | bytes 1048576

commit v5 on v4

--- a/solution.py
+++ b/solution.py
@@ -224,12 +224,13 @@
 
     hid_copies = [hid_copy(part) for part in range(4)]
 
-    def hid_start():
-        @pl.when((zh == 0) & (core == 1))
-        def _():
-            pl.semaphore_wait(hid_ready, 1)
-
-        @pl.when(p < 31)
+    def hid_start(half):
+        if half == 0:
+            @pl.when((zh == 0) & (core == 1))
+            def _():
+                pl.semaphore_wait(hid_ready, 1)
+
+        @pl.when((zh == half) & (p < 31))
         def _():
             for copy in hid_copies:
                 copy.start()
@@ -327,8 +328,6 @@
         def _():
             az_copy(b).start()
 
-        if b == 1:
-            wx_pass(1, 1)
 
     def ay_copy(way, hop, sub):
         block = ring(y - hop + 1) if way == 0 else ring(y + hop - 1)
@@ -376,23 +375,25 @@
         lax.fori_loop(0, RING, one, 0)
 
     ay_first(0)
+    wx_pass(1, 1)
+    ay_first(1)
     wx_pass(1, 2)
-    ay_first(1)
     ay_pass(1, 0)
+    ay_first(2)
     wx_pass(2, 0)
-    ay_first(2)
     ay_pass(1, 1)
     wx_pass(2, 1)
     ay_pass(2, 0)
     ay_pass(1, 2)
     wx_pass(2, 2)
     ay_first(3)
-    hid_start()
+    hid_start(1)
     ay_pass(2, 1)
     wx_pass(3, 0)
     ay_pass(2, 2)
     ay_pass(3, 0)
     ay_pass(1, 3)
+    hid_start(0)
     wx_pass(3, 1)
     ay_pass(3, 1)
     ay_pass(2, 3)

time: 65.4 us -> 66.7 us (1.020)
  the two profiles are of different devices: /device:TPU:2 before, /device:TPU:14 now
where the time goes in v5:
time: 66.7 us; the launch traced here: 66.5 us
  Pallas kernels  65.7 us (99%)
  local copies, waits for them, and re-layouts  0.8 us (1%)
    pallas_call x1, Pallas kernels, on_device(): pl.pallas_call(kernel, out_shape=jax.ShapeDtypeStruct((rows, width), BF16...  65.7 us

profile of v5, /device:TPU:14, one launch (start us, length us, event | category | flops | bytes accessed | tf_op | source)
XLA Modules:
  0.0 66.5 jit_solution(10911480454171504658)
XLA Ops:
  0.0 65.7 %shard_map.73 = bf16[256,1024]{1,0:T(8,128)(2,1)S(1)} custom-call(bf16[128,1024]{1,0:T(8,128)(2,1)} %bitcast.9, bf16[128,128]{1,0:T(8,128)(2,1)} %bitcast.10, bf16[128,128]{1,0:T(8,128)(2,1)} %bitcast.11, s32[1,1024]{1,0:T(1,128)} %seg_in.1, bf16[8,128,1024]{2,1,0:T(8,128)(2,1)} %bitcast.7, bf16[256,1024]{1,0:T(8,128)(2,1)} %emb_ref.1, bf16[256,1024]{1,0:T(8,128)(2,1)} %bitcast.8), custom_call_target="tpu_custom_call" | custom-call | tf_op jit(solution)/shard_map/pallas_call | solution.py:448
  65.7 0.8 %copy.9 = bf16[1,256,1024]{2,1,0:T(8,128)(2,1)} copy(bf16[1,256,1024]{2,1,0:T(8,128)(2,1)S(1)} %bitcast.6) | data formatting | bytes 1048576
